TPU v7x, 512 devices: a whole 4x8x8 slice. The times are simulated.
512 devices in a mesh: rep: 64 (over z, y_lo, x), fsdp: 8 (over y_hi, core).
Axes of the slice: x: 4, y: 8 (y_hi: 4, y_lo: 2; y = y_hi * 2 + y_lo), z: 8, core: 2. Of those that a mesh axis runs over, the one named last changes fastest.
Arguments:
- deltas: bfloat16 [64, 57344, 128], P('rep', 'fsdp'), may hold values from -1 to 1
- scales: bfloat16 [64, 57344], P('rep', 'fsdp'), may hold values from 0.1 to 30, as said below
- clip_level: float32 [], replicated, may hold values from 0.02 to 0.05
- master: float32 [57344, 128], P(('fsdp', 'rep')), may hold values from -6 to 6
- momentum: float32 [57344, 128], P(('fsdp', 'rep')), may hold values from -0.75 to 0.75
Outputs:
- new_base: bfloat16 [256, 28672], P('fsdp')
- new_master: float32 [57344, 128], P(('fsdp', 'rep'))
- new_momentum: float32 [57344, 128], P(('fsdp', 'rep'))
Inputs may be any that keep to these rules, and one draw needn't show every extreme that they name: `scales`: positive.
All inputs are finite; a program needn't handle non-finite values.
Results may differ from a plain program's by a relative error of at most 0.0004.
Values may be sent and summed in bfloat16 or wider, within the bound.
A program may use at most 64 MiB of HBM per device.

v0:
```python
import math

import jax
import jax.numpy as jnp
from jax import lax
from jax.sharding import Mesh
from jax.sharding import PartitionSpec as P

FF = 28672
REP = ("rep_0", "rep_1", "rep_2")
REP_FSDP = ("rep_0", "rep_1", "rep_2", "fsdp_0", "fsdp_1")
FSDP = ("fsdp_0", "fsdp_1")
FSDP_REP = ("fsdp_0", "fsdp_1", "rep_0", "rep_1", "rep_2")


def sent_together(arrays, axis, split_dim, concat_dim, along):
    widths = [math.prod(a.shape[along:]) for a in arrays]
    both = jnp.concatenate(
        [a.reshape(*a.shape[:along], w) for a, w in zip(arrays, widths)], axis=along
    )
    result = lax.all_to_all(both, axis, split_axis=split_dim, concat_axis=concat_dim, tiled=True)
    pieces = jnp.split(result, [sum(widths[:k]) for k in range(1, len(widths))], axis=along)
    return tuple(
        (b.reshape(*result.shape[:along], *a.shape[along:]) for a, b in zip(arrays, pieces))
    )


def by_axis(array, axes):
    for axis in axes:
        array = lax.psum(array, axis)
    return array


def copy_for_each(array, axis):
    copies = jnp.broadcast_to(array, (lax.axis_size(axis), *array.shape))
    return lax.all_to_all(copies, axis, split_axis=0, concat_axis=0, tiled=True)


def joined_along(pieces, dim):
    pieces = jnp.moveaxis(pieces, 0, dim)
    lengths = pieces.shape
    return pieces.reshape(*lengths[:dim], lengths[dim] * lengths[dim + 1], *lengths[dim + 2 :])


def collect(array, axis, dim):
    pieces = copy_for_each(array, axis)
    return joined_along(pieces, dim)


def per_device(deltas, scales, clip_level, master, momentum):
    replicas = lax.axis_size(REP)
    values, factors = sent_together((deltas, scales), REP, 1, 0, 2)
    decoded = values.astype(jnp.float32) * factors.astype(jnp.float32)[:, :, None]
    outer_grad = jnp.sum(decoded, axis=0) / replicas
    squares = by_axis(jnp.sum(outer_grad * outer_grad), REP_FSDP)
    entries = outer_grad.size * replicas * lax.axis_size(FSDP)
    factor = jnp.minimum(1.0, clip_level / jnp.sqrt(squares / entries + 1e-06))
    new_momentum = 0.9 * momentum + factor * outer_grad
    new_master = master - 0.7 * (factor * outer_grad + 0.9 * new_momentum)
    owned_piece = new_master.astype(jnp.bfloat16)
    gathered = collect(owned_piece, REP, 0)
    new_base = gathered.reshape(-1, FF)
    return (new_base, new_master, new_momentum)


def solution(mesh):
    finer = Mesh(
        mesh.devices.reshape(8, 2, 4, 4, 2), ("rep_0", "rep_1", "rep_2", "fsdp_0", "fsdp_1")
    )
    in_specs = (P(REP, FSDP, None), P(REP, FSDP), P(), P(FSDP_REP, None), P(FSDP_REP, None))
    out_specs = (P(FSDP, None), P(FSDP_REP, None), P(FSDP_REP, None))
    return jax.shard_map(
        per_device, mesh=finer, in_specs=in_specs, out_specs=out_specs, check_vma=False
    )
```

profile of v0, /device:TPU:6, one launch (start us, length us, event | category | flops | bytes accessed | tf_op | source)
XLA Modules:
  0.0 281.4 jit_solution(1563916486025639491)
XLA Ops:
  0.6 0.0 copy-start.2
  0.6 6.8 %copy.26 = bf16[1,7168,128]{2,0,1:T(2,128)(2,1)} copy(bf16[1,7168,128]{2,1,0:T(8,128)(2,1)} %param.5) | data formatting | bytes 3670016 | tf_op args[0]
  7.4 0.0 copy-done.2
  7.4 6.0 %copy.27 = bf16[1,7168,1]{2,0,1:T(2,128)(2,1)} copy(bf16[1,7168,1]{1,2,0:T(2,128)(2,1)S(1)} %bitcast.12) | data formatting | bytes 28672 | tf_op jit(solution)/shard_map/reshape | solution.py:19
  13.4 12.3 %fusion.2 = bf16[7168,1,129]{2,1,0:T(2,128)(2,1)} fusion(bf16[1,7168,1]{2,0,1:T(2,128)(2,1)} %copy.27, bf16[1,7168,128]{2,0,1:T(2,128)(2,1)} %copy.26), kind=kLoop, calls=%fused_computation.8 | loop fusion | flops 3698688 | bytes 3698688
  25.7 0.5 broadcast.11
  26.3 42.1 %reduce = bf16[7168,129]{1,0:T(8,128)(2,1)} reduce(bf16[7168,1,129]{2,1,0:T(2,128)(2,1)} %fusion.2, bf16[]{:T(256)} %broadcast.11), dimensions={1}, to_apply=%fusion.2.reduce_sub_computation | reduce | bytes 3698690
  68.3 7.9 %reshape.15 = bf16[64,2,7224]{2,1,0:T(2,128)(2,1)S(1)} reshape(bf16[7168,129]{1,0:T(8,128)(2,1)} %reduce) | data formatting | bytes 3698688
  76.2 60.3 %all_to_all.17 = bf16[64,2,7224]{2,1,0:T(2,128)(2,1)} all-to-all(bf16[64,2,7224]{2,1,0:T(2,128)(2,1)S(1)} %reshape.15), channel_id=1, replica_groups=mesh['rep_0'=8,'rep_1'=2,'rep_2'=4,'fsdp_0'=4,'fsdp_1'=2] {'rep_0','rep_..., dimensions={0} | all-to-all | bytes 3698688 | tf_op jit(solution)/shard_map/all_to_all | solution.py:21
  136.6 19.6 %reshape.16 = bf16[7168,1,129]{2,1,0:T(2,128)(2,1)} reshape(bf16[64,2,7224]{2,1,0:T(2,128)(2,1)} %all_to_all.17) | data formatting | bytes 3698688
  156.2 15.5 %copy.28 = bf16[1,7168,129]{1,2,0:T(8,128)(2,1)} copy(bf16[1,7168,129]{2,0,1:T(2,128)(2,1)} %bitcast.11) | data formatting | bytes 3698688 | tf_op jit(solution)/shard_map/all_to_all | solution.py:21
  171.6 0.0 copy-start
  171.6 0.0 copy-start.1
  171.6 4.2 %all_to_all.13 = bf16[64,112,129]{1,0,2:T(8,128)(2,1)S(1)} reshape(bf16[1,7168,129]{1,2,0:T(8,128)(2,1)} %copy.28) | data formatting | bytes 3698688 | tf_op jit(solution)/shard_map/all_to_all | solution.py:21
  175.8 0.8 multiply_reduce_fusion
  176.6 0.6 multiply_reduce_fusion.1
  177.2 15.2 %psum.35 = f32[]{:T(128)} all-reduce(f32[]{:T(128)} %multiply_reduce_fusion.1), channel_id=1, replica_groups=mesh['rep_0'=8,'rep_1'=2,'rep_2'=4,'fsdp_0'=4,'fsdp_1'=2] {'rep_0'}, use_global_device_ids=true, to_apply=%region_2.0 | all-reduce | flops 1 | bytes 8 | tf_op jit(solution)/shard_map/psum | solution.py:30
  192.5 5.5 %psum.36 = f32[]{:T(128)} all-reduce(f32[]{:T(128)} %psum.35), channel_id=1, replica_groups=mesh['rep_0'=8,'rep_1'=2,'rep_2'=4,'fsdp_0'=4,'fsdp_1'=2] {'rep_1'}, use_global_device_ids=true, to_apply=%region_3.0 | all-reduce | flops 1 | bytes 8 | tf_op jit(solution)/shard_map/psum | solution.py:30
  198.7 8.3 %psum.37 = f32[]{:T(128)} all-reduce(f32[]{:T(128)} %psum.36), channel_id=1, replica_groups=mesh['rep_0'=8,'rep_1'=2,'rep_2'=4,'fsdp_0'=4,'fsdp_1'=2] {'rep_2'}, use_global_device_ids=true, to_apply=%region_4.0 | all-reduce | flops 1 | bytes 8 | tf_op jit(solution)/shard_map/psum | solution.py:30
  207.0 0.0 copy-done
  207.0 0.1 copy.29
  207.1 12.6 %psum.38 = f32[]{:T(128)} all-reduce(f32[]{:T(128)} %psum.37), channel_id=1, replica_groups=mesh['rep_0'=8,'rep_1'=2,'rep_2'=4,'fsdp_0'=4,'fsdp_1'=2] {'fsdp_0'}, use_global_device_ids=true, to_apply=%region_5.0 | all-reduce | flops 1 | bytes 8 | tf_op jit(solution)/shard_map/psum | solution.py:30
  219.7 0.0 copy-done.1
  219.7 0.1 copy.30
  219.8 3.1 %psum.39 = f32[]{:T(128)} all-reduce(f32[]{:T(128)} %psum.38), channel_id=1, replica_groups=mesh['rep_0'=8,'rep_1'=2,'rep_2'=4,'fsdp_0'=4,'fsdp_1'=2] {'fsdp_1'}, use_global_device_ids=true, to_apply=%region_6.0 | all-reduce | flops 1 | bytes 8 | tf_op jit(solution)/shard_map/psum | solution.py:30
  223.6 0.1 copy.31
  223.7 1.5 broadcast_in_dim.4
  225.2 9.3 %all-to-all-start.1 = ((bf16[64,112,128]{2,1,0:T(8,128)(2,1)}), bf16[64,112,128]{2,1,0:T(8,128)(2,1)S(1)}, u32[]{:S(2)}, u32[]{:S(2)}) async-start(bf16[64,112,128]{2,1,0:T(8,128)(2,1)} %broadcast_in_dim.4), calls=%async_computation.1 | async-start | bytes 3670016 | tf_op jit(solution)/shard_map/all_to_all | solution.py:36
  234.6 0.7 copy.32
  235.3 0.7 copy.33
  236.0 43.7 %all-to-all-done.1 = bf16[64,112,128]{2,1,0:T(8,128)(2,1)S(1)} async-done(((bf16[64,112,128]{2,1,0:T(8,128)(2,1)}), bf16[64,112,128]{2,1,0:T(8,128)(2,1)S(1)}, u32[]{:S(2)}, u32[]{:S(2)}) %all-to-all-start.1) | async-done | bytes 1835040 | tf_op jit(solution)/shard_map/all_to_all | solution.py:36
  279.6 1.7 reshape_reshape.3
  (2 shorter events, 0.0 us)
Async XLA Ops:
  0.6 6.8 %copy-start.2 = (bf16[1,7168]{1,0:T(2,128)(2,1)S(1)}, bf16[1,7168]{1,0:T(2,128)(2,1)}, u32[]{:S(2)}) copy-start(bf16[1,7168]{1,0:T(2,128)(2,1)} %param.6) | copy-start | bytes 43012
  171.6 35.3 %copy-start = (f32[112,128]{1,0:T(8,128)S(1)}, f32[112,128]{1,0:T(8,128)}, u32[]{:S(2)}) copy-start(f32[112,128]{1,0:T(8,128)} %param.9) | copy-start | bytes 172036
  171.6 48.1 %copy-start.1 = (f32[112,128]{1,0:T(8,128)S(1)}, f32[112,128]{1,0:T(8,128)}, u32[]{:S(2)}) copy-start(f32[112,128]{1,0:T(8,128)} %param.8) | copy-start | bytes 172036
  225.2 54.4 %all-to-all-start.1 = ((bf16[64,112,128]{2,1,0:T(8,128)(2,1)}), bf16[64,112,128]{2,1,0:T(8,128)(2,1)S(1)}, u32[]{:S(2)}, u32[]{:S(2)}) async-start(bf16[64,112,128]{2,1,0:T(8,128)(2,1)} %broadcast_in_dim.4), calls=%async_computation.1 | async-start | bytes 3670016 | tf_op jit(solution)/shard_map/all_to_all | solution.py:36
where the time goes:
time: 284 us; the launch traced here: 281 us
  blocking collectives  105 us (37%)
  local copies, waits for them, and re-layouts  65.3 us (23%)
  other arithmetic  55.8 us (20%)
  waiting for transfers between devices  43.7 us (15%)
  starting transfers between devices  9.33 us (3%)
    all_to_all x1, blocking collectives, sent_together(): lax.all_to_all(both, axis, split_axis=split_dim, concat_axis=concat_dim,...  60.3 us
    unnamed x2, other arithmetic  54.4 us
    psum x5, blocking collectives, by_axis(): array = lax.psum(array, axis)  44.8 us
    all_to_all x1, waiting for transfers between devices, copy_for_each(): return lax.all_to_all(copies, axis, split_axis=0, concat_axis=0, tiled=True)  43.7 us
    unnamed x14, local copies, waits for them, and re-layouts  36.4 us
    all_to_all x2, local copies, waits for them, and re-layouts, sent_together(): lax.all_to_all(both, axis, split_axis=split_dim, concat_axis=concat_dim,...  19.6 us
    all_to_all x1, starting transfers between devices, copy_for_each(): return lax.all_to_all(copies, axis, split_axis=0, concat_axis=0, tiled=True)  9.33 us
    reshape x1, local copies, waits for them, and re-layouts, sent_together(): a.reshape(*a.shape[:along], w)  5.99 us
  transfers between devices with their start and end apart: 1, of which 1 were waited for; matrix products, arithmetic and copies ran while one was open for 1% of the time, Pallas kernels for 0%

commit v1 on v0

v1 whole, which is shorter than its diff:
```python
import functools

import jax
import jax.numpy as jnp
from jax import lax
from jax.experimental import pallas as pl
from jax.experimental.pallas import tpu as pltpu
from jax.sharding import PartitionSpec as P

FF = 28672
MESH = pl.DeviceIdType.MESH
NX, NY, NZ = 4, 2, 8
ROWS = 112
PAD = 128
ORDER = (4, 3, 5, 2, 6, 1, 7, 0)
BF16, F32 = jnp.bfloat16, jnp.float32


def kernel(
    deltas, scales, clip, master, momentum,
    gathered, grad_out, factor_out,
    rx, table, table16, rs, sf, ysrc, yrx, zsrc, zrx, acc, a_own, az, gz, nb, sq, ar_rx,
    local_sem, xs, xr, ss, sr, ys, yr, zs, zr, as_, ar, gs, gr, qs, qr, bs, br,
):
    rep, fsdp = lax.axis_index("rep"), lax.axis_index("fsdp")
    x, yl, z = lax.rem(rep, 4), lax.rem(rep // 4, 2), rep // 8
    yh, core = fsdp // 2, lax.rem(fsdp, 2)
    y = yh * 2 + yl

    def device(x, yl, z):
        return ((z * 2 + yl) * 4 + x, fsdp)

    def along_x(d):
        return device(lax.rem(x + d, 4), yl, z)

    def along_z(d):
        return device(x, yl, lax.rem(z + d, 8))

    y_peer = device(x, 1 - yl, z)

    def along_xc(d):
        other = lax.rem(core + d // 4, 2)
        return ((z * 2 + yl) * 4 + lax.rem(x + d % 4, 4), yh * 2 + other)

    def along_y(d):
        to = lax.rem(y + d, 8)
        return ((z * 2 + lax.rem(to, 2)) * 4 + x, (to // 2) * 2 + core)

    barrier = pltpu.get_barrier_semaphore()
    for d in range(1, 8):
        for peer in (along_z(d), along_xc(d), along_y(d)):
            pl.semaphore_signal(barrier, inc=1, device_id=peer, device_id_type=MESH)

    own = pltpu.make_async_copy(deltas.at[:, x], rx.at[:, x, pl.ds(0, ROWS)], local_sem)
    own.start()
    a_own[...] = master[...] - 0.567 * momentum[...]
    pl.semaphore_wait(barrier, 21)

    def remote(src, dst, send, recv, to):
        copy = pltpu.make_async_remote_copy(
            src_ref=src, dst_ref=dst, send_sem=send, recv_sem=recv, device_id=to, device_id_type=MESH
        )
        copy.start()
        return copy

    xcopies = []
    for s, dz in enumerate(ORDER):
        to = lax.rem(z + dz, 8)
        copies = []
        for k, d in enumerate((2, 1, 3)):
            xd = lax.rem(x + d, 4)
            copies.append(
                remote(
                    deltas.at[pl.ds(2 * to, 2), xd], rx.at[pl.ds(2 * to, 2), x, pl.ds(0, ROWS)],
                    xs.at[s, k], xr.at[s, k], along_x(d),
                )
            )
        xcopies.append(copies)
        if s == 0:
            flat = scales[...].astype(F32)
            for r in range(NX * NY * NZ):
                table[r % 4, r // 4 : r // 4 + 1, 0:ROWS] = flat[:, ROWS * r : ROWS * (r + 1)]
            for k in range(4):
                table16[k] = table[k].astype(BF16)
            scopies = [
                remote(table16.at[lax.rem(x + d, 4)], rs.at[x], ss.at[k], sr.at[k], along_x(d))
                for k, d in enumerate((2, 1, 3))
            ]
    acopies = [remote(a_own, az.at[z], as_.at[d - 1], ar.at[d - 1], along_z(d)) for d in range(1, 8)]

    for zy in range(16):
        for k in range(4):
            rx[zy, k, ROWS:PAD] = jnp.zeros((PAD - ROWS, 128), BF16)
    for copy in scopies:
        copy.wait()
    for k in range(4):
        sf[k] = rs[k].astype(F32)
    sf[x] = table[x]
    own.wait()

    eye = lax.broadcasted_iota(jnp.int32, (ROWS, PAD), 0) == lax.broadcasted_iota(jnp.int32, (ROWS, PAD), 1)

    def decode(zy):
        diags = [
            jnp.where(eye, jnp.broadcast_to(sf[k, pl.ds(zy, 1), :], (ROWS, PAD)), 0.0).astype(BF16)
            for k in range(4)
        ]
        return jnp.dot(
            jnp.concatenate(diags, axis=1), rx[zy].reshape(4 * PAD, 128), preferred_element_type=F32
        )

    ycopies, zcopies = [], []

    def finish(s):
        ycopies[s].wait()
        total = acc[s] + yrx[s]
        if ORDER[s] == 0:
            acc[s] = total
        else:
            zsrc[s] = total
            zcopies.append(
                remote(zsrc.at[s], zrx.at[s], zs.at[s], zr.at[s], along_z(ORDER[s]))
            )

    for s, dz in enumerate(ORDER):
        to = lax.rem(z + dz, 8)
        for copy in xcopies[s]:
            copy.wait()
        ysrc[s] = decode(2 * to + 1 - yl)
        ycopies.append(remote(ysrc.at[s], yrx.at[s], ys.at[s], yr.at[s], y_peer))
        acc[s] = decode(2 * to + yl)
        if s > 0:
            finish(s - 1)
    finish(7)
    total = acc[7]
    for s in range(7):
        zcopies[s].wait()
        total = total + zrx[s]
    grad = total * (1.0 / (NX * NY * NZ))
    grad_out[...] = grad
    gz[z] = grad
    partial = jnp.sum((grad * grad).reshape(ROWS // 8, 8, 128), axis=0)
    sq[0] = partial
    gcopies = None
    for stage, way in enumerate((along_xc, along_y, along_z)):
        copies = [
            remote(sq.at[stage], ar_rx.at[stage, d - 1], qs.at[stage, d - 1], qr.at[stage, d - 1], way(d))
            for d in range(1, 8)
        ]
        if gcopies is None:
            gcopies = [remote(gz.at[z], gz.at[z], gs.at[d - 1], gr.at[d - 1], along_z(d)) for d in range(1, 8)]
        for d in range(7):
            copies[d].wait()
            partial = partial + ar_rx[stage, d]
        if stage < 2:
            sq[stage + 1] = partial
    mean = jnp.sum(jnp.sum(partial, axis=1, keepdims=True), axis=0, keepdims=True) * (1.0 / (512 * ROWS * 128))
    factor = jnp.minimum(1.0, clip[0, 0] / jnp.sqrt(mean + 1e-06))
    factor_out[...] = jnp.broadcast_to(factor, (8, 128))
    for copy in acopies + gcopies:
        copy.wait()
    az[z] = a_own[...]
    step = 1.33 * factor

    def send_base(zi, to, i):
        here = nb.at[zi]
        return remote(here, gathered.at[zi, yl, x], bs.at[i], br.at[i], to)

    first = []
    n = 0
    for zi in (0, 4, 1, 5, 2, 6, 3, 7):
        nb[zi] = (az[zi] - step * gz[zi]).astype(BF16)
        if zi < 4:
            for d in (2, 1, 3):
                first.append((zi, d, send_base(zi, along_x(d), n)))
                n += 1
        else:
            first.append((zi, 0, send_base(zi, y_peer, n)))
            n += 1
    second = []
    for zi in (0, 1, 2, 3):
        second.append(send_base(zi, y_peer, n))
        n += 1
        for d in (2, 1, 3):
            second.append(send_base(zi + 4, along_x(d), n))
            n += 1
    for zi, d, copy in first:
        copy.wait()
        if zi < 4:
            source = lax.rem(x + 4 - d, 4)
            block = gathered.at[zi, yl, source]
            second.append(remote(block, block, bs.at[n], br.at[n], y_peer))
            n += 1
        else:
            block = gathered.at[zi, 1 - yl, x]
            for d in (2, 1, 3):
                second.append(remote(block, block, bs.at[n], br.at[n], along_x(d)))
                n += 1
    whole = pltpu.make_async_copy(nb, gathered.at[:, yl, x], local_sem)
    whole.start()
    whole.wait()
    for copy in second:
        copy.wait()


def finish_kernel(gathered, grad, factor, master, momentum, base, new_master, new_momentum, wide):
    wide[...] = gathered[...].reshape(16 * ROWS, 128).astype(F32)
    for j in range(ROWS):
        base[:, 128 * j : 128 * (j + 1)] = wide[pl.ds(j, 16, stride=ROWS), :].astype(BF16)

    @pl.when((pl.program_id(0) == 0) & (pl.program_id(1) == 0))
    def _():
        scaled = factor[0:1, 0:1] * grad[...]
        moved = 0.9 * momentum[...] + scaled
        new_momentum[...] = moved
        new_master[...] = master[...] - 0.7 * (scaled + 0.9 * moved)


def per_device(deltas, scales, clip_level, master, momentum):
    vmem, anywhere = pl.BlockSpec(memory_space=pltpu.VMEM), pl.BlockSpec(memory_space=pl.ANY)
    dma = pltpu.SemaphoreType.DMA
    gathered, grad, factor = pl.pallas_call(
        kernel,
        out_shape=(
            jax.ShapeDtypeStruct((NZ, NY, NX, ROWS, 128), BF16),
            jax.ShapeDtypeStruct((ROWS, 128), F32),
            jax.ShapeDtypeStruct((8, 128), F32),
        ),
        in_specs=[anywhere, vmem, pl.BlockSpec(memory_space=pltpu.SMEM), vmem, vmem],
        out_specs=(anywhere, vmem, vmem),
        scratch_shapes=[
            pltpu.VMEM((NZ * NY, NX, PAD, 128), BF16),
            pltpu.VMEM((NX, NZ * NY, 128), F32),
            pltpu.VMEM((NX, NZ * NY, 128), BF16),
            pltpu.VMEM((NX, NZ * NY, 128), BF16),
            pltpu.VMEM((NX, NZ * NY, 128), F32),
            pltpu.VMEM((NZ, ROWS, 128), F32),
            pltpu.VMEM((NZ, ROWS, 128), F32),
            pltpu.VMEM((NZ, ROWS, 128), F32),
            pltpu.VMEM((NZ, ROWS, 128), F32),
            pltpu.VMEM((NZ, ROWS, 128), F32),
            pltpu.VMEM((ROWS, 128), F32),
            pltpu.VMEM((NZ, ROWS, 128), F32),
            pltpu.VMEM((NZ, ROWS, 128), F32),
            pltpu.VMEM((NZ, ROWS, 128), BF16),
            pltpu.VMEM((3, 8, 128), F32),
            pltpu.VMEM((3, 7, 8, 128), F32),
            dma,
            dma((8, 3)), dma((8, 3)),
            dma((3,)), dma((3,)),
            dma((8,)), dma((8,)),
            dma((8,)), dma((8,)),
            dma((7,)), dma((7,)),
            dma((7,)), dma((7,)),
            dma((3, 7)), dma((3, 7)),
            dma((56,)), dma((56,)),
        ],
        compiler_params=pltpu.CompilerParams(
            collective_id=0, has_side_effects=True, vmem_limit_bytes=40 * 2**20
        ),
    )(
        deltas.reshape(NZ * NY, NX, ROWS, 128), scales, clip_level.reshape(1, 1), master, momentum
    )
    small = lambda shape: pl.BlockSpec(shape, lambda h, i: (0, 0))
    return pl.pallas_call(
        finish_kernel,
        grid=(2, 2),
        out_shape=(
            jax.ShapeDtypeStruct((32, FF), BF16),
            jax.ShapeDtypeStruct((ROWS, 128), F32),
            jax.ShapeDtypeStruct((ROWS, 128), F32),
        ),
        in_specs=[
            pl.BlockSpec((16, None, ROWS, 128), lambda h, i: (i, h, 0, 0)),
            small((ROWS, 128)), small((8, 128)), small((ROWS, 128)), small((ROWS, 128)),
        ],
        out_specs=(
            pl.BlockSpec((16, FF // 2), lambda h, i: (i, h)), small((ROWS, 128)), small((ROWS, 128)),
        ),
        scratch_shapes=[pltpu.VMEM((16 * ROWS, 128), F32)],
    )(gathered.reshape(32, 2, ROWS, 128), grad, factor, master, momentum)


def solution(mesh):
    fr = ("fsdp", "rep")
    in_specs = (P("rep", "fsdp", None), P("rep", "fsdp"), P(), P(fr, None), P(fr, None))
    out_specs = (P("fsdp", None), P(fr, None), P(fr, None))
    return jax.shard_map(
        per_device, mesh=mesh, in_specs=in_specs, out_specs=out_specs, check_vma=False
    )
```

time: 284 us -> 87.2 us (0.31)
  blocking collectives: 105 us -> 0 us
  Pallas kernels: 0 us -> 77.9 us
  local copies, waits for them, and re-layouts: 65.3 us -> 6.31 us
  other arithmetic: 55.8 us -> 0 us
  waiting for transfers between devices: 43.7 us -> 0 us
  starting transfers between devices: 9.33 us -> 0 us
    pallas_call x0 -> x2, Pallas kernels: none -> 77.9 us  [the longest x1 73.5 us: per_device(): pl.pallas_call(kernel, out_shape=(jax.ShapeDtypeStruct((NZ, NY, NX, ROWS,...]
    all_to_all x1 -> x0, blocking collectives: 60.3 us -> none  [sent_together(): lax.all_to_all(both, axis, split_axis=split_dim, concat_axis=concat_dim,...]
    unnamed x2 -> x0, other arithmetic: 54.4 us -> none
    psum x5 -> x0, blocking collectives: 44.8 us -> none  [by_axis(): array = lax.psum(array, axis)]
    all_to_all x1 -> x0, waiting for transfers between devices: 43.7 us -> none  [copy_for_each(): return lax.all_to_all(copies, axis, split_axis=0, concat_axis=0, tiled=True)]
    unnamed x14, local copies, waits for them, and re-layouts: 36.4 us -> 6.31 us
    all_to_all x2 -> x0, local copies, waits for them, and re-layouts: 19.6 us -> none  [sent_together(): lax.all_to_all(both, axis, split_axis=split_dim, concat_axis=concat_dim,...]
    all_to_all x1 -> x0, starting transfers between devices: 9.33 us -> none  [copy_for_each(): return lax.all_to_all(copies, axis, split_axis=0, concat_axis=0, tiled=True)]
  transfers between devices with their start and end apart: 1 -> 0, of which waited for: 1 -> 0; matrix products, arithmetic and copies ran while one was open for 1% -> 0% of each run, Pallas kernels for 0% -> 0%
where the time goes in v1:
time: 87.2 us; the launch traced here: 85.5 us
  Pallas kernels  77.9 us (89%)
  local copies, waits for them, and re-layouts  6.31 us (7%)
  between operations  1.31 us (2%)
    pallas_call x1, Pallas kernels, per_device(): pl.pallas_call(kernel, out_shape=(jax.ShapeDtypeStruct((NZ, NY, NX, ROWS,...  73.5 us
    unnamed x14, local copies, waits for them, and re-layouts  6.31 us
    pallas_call x1, Pallas kernels, per_device(): pl.pallas_call(finish_kernel, grid=(2, 2), out_shape=(jax.ShapeDtypeStruc...  4.39 us

profile of v1, /device:TPU:6, one launch (start us, length us, event | category | flops | bytes accessed | tf_op | source)
XLA Modules:
  0.0 85.5 jit_solution(7985716140425829935)
XLA Ops:
  1.3 0.0 copy-start
  1.3 1.5 %copy-done = bf16[1,7168,128]{2,1,0:T(8,128)(2,1)S(1)} copy-done((bf16[1,7168,128]{2,1,0:T(8,128)(2,1)S(1)}, bf16[1,7168,128]{2,1,0:T(8,128)(2,1)}, u32[]{:S(2)}) %copy-start) | copy-done | bytes 1835032
  2.8 0.0 copy-start.2
  2.8 0.8 copy-done.2
  3.6 0.0 copy-start.3
  3.6 0.8 copy-done.3
  4.4 0.0 copy-start.5
  4.4 0.7 copy-done.5
  5.2 73.5 %shard_map.76 = (bf16[8,2,4,112,128]{4,3,2,1,0:T(8,128)(2,1)S(1)}, f32[112,128]{1,0:T(8,128)S(1)}, f32[8,128]{1,0:T(8,128)S(1)}) custom-call(bf16[16,4,112,128]{3,2,1,0:T(8,128)(2,1)S(1)} %bitcast.4, bf16[1,7168]{1,0:T(2,128)(2,1)S(1)} %copy-done.5, f32[1,1]{1,0:T(1,128)} %bitcast.3.clip, f32[112,128]{1,0:T(8,128)S(1)} %copy-done.2, f32[112,128]{1,0:T(8,128)S(1)} %copy-done.3), custom_call_target="tpu_custom_call" | custom-call | tf_op jit(solution)/shard_map/pallas_call | solution.py:222
  78.7 0.0 copy-start.1
  78.7 1.2 %copy-done.1 = bf16[8,2,4,112,128]{4,3,2,1,0:T(8,128)(2,1)} copy-done((bf16[8,2,4,112,128]{4,3,2,1,0:T(8,128)(2,1)}, bf16[8,2,4,112,128]{4,3,2,1,0:T(8,128)(2,1)S(1)}, u32[]{:S(2)}) %copy-start.1) | copy-done | bytes 1835032
  79.9 0.0 copy-start.4
  79.9 0.6 copy-done.4
  80.5 0.0 copy-start.6
  80.5 0.6 copy-done.6
  81.1 4.4 %shard_map.77 = (bf16[32,28672]{1,0:T(8,128)(2,1)}, f32[112,128]{1,0:T(8,128)}, f32[112,128]{1,0:T(8,128)}) custom-call(bf16[32,2,112,128]{3,2,1,0:T(8,128)(2,1)} %bitcast.5, f32[112,128]{1,0:T(8,128)} %copy-done.4, f32[8,128]{1,0:T(8,128)} %copy-done.6, f32[112,128]{1,0:T(8,128)} %master.3, f32[112,128]{1,0:T(8,128)} %momentum.3), custom_call_target="tpu_custom_call" | custom-call | tf_op jit(solution)/shard_map/pallas_call | solution.py:265
Async XLA Ops:
  1.3 1.5 %copy-start = (bf16[1,7168,128]{2,1,0:T(8,128)(2,1)S(1)}, bf16[1,7168,128]{2,1,0:T(8,128)(2,1)}, u32[]{:S(2)}) copy-start(bf16[1,7168,128]{2,1,0:T(8,128)(2,1)} %param.5) | copy-start | bytes 5505028
  2.8 0.8 copy-start.2
  3.6 0.8 copy-start.3
  4.4 0.7 copy-start.5
  78.7 1.2 %copy-start.1 = (bf16[8,2,4,112,128]{4,3,2,1,0:T(8,128)(2,1)}, bf16[8,2,4,112,128]{4,3,2,1,0:T(8,128)(2,1)S(1)}, u32[]{:S(2)}) copy-start(bf16[8,2,4,112,128]{4,3,2,1,0:T(8,128)(2,1)S(1)} %get-tuple-element.6) | copy-start | bytes 5505028
  79.9 0.6 copy-start.4
  80.5 0.6 copy-start.6

commit v2 on v1

v2 whole, which is shorter than its diff:
```python
import functools

import jax
import jax.numpy as jnp
from jax import lax
from jax.experimental import pallas as pl
from jax.experimental.pallas import tpu as pltpu
from jax.sharding import PartitionSpec as P

FF = 28672
MESH = pl.DeviceIdType.MESH
NX, NY, NZ = 4, 2, 8
ROWS = 112
PAD = 128
SEQUENCE = (
    (0, 4), (0, 3), (0, 5), (1, 4), (0, 2), (1, 3), (0, 6), (1, 5),
    (0, 1), (0, 7), (0, 0), (1, 2), (1, 6), (1, 1), (1, 7), (1, 0),
)
BF16, F32 = jnp.bfloat16, jnp.float32


def kernel(
    deltas, scales, clip, master, momentum,
    gathered, grad_out, factor_out,
    scales_v, clip_v, master_v, momentum_v, rx, table, table16, rs, sf, ysrc, yrx, zsrc, zrx, az, gz, nb, sq, ar_rx,
    own_sem, in_sem, xs, xr, ss, sr, ys, yr, zs, zr, as_, ar, gs, gr, qs, qr, bs, br,
):
    rep, fsdp = lax.axis_index("rep"), lax.axis_index("fsdp")
    x, yl, z = lax.rem(rep, 4), lax.rem(rep // 4, 2), rep // 8
    yh, core = fsdp // 2, lax.rem(fsdp, 2)
    y = yh * 2 + yl

    def device(x, yl, z):
        return ((z * 2 + yl) * 4 + x, fsdp)

    def along_x(d):
        return device(lax.rem(x + d, 4), yl, z)

    def along_z(d):
        return device(x, yl, lax.rem(z + d, 8))

    y_peer = device(x, 1 - yl, z)

    def along_xc(d):
        other = lax.rem(core + d // 4, 2)
        return ((z * 2 + yl) * 4 + lax.rem(x + d % 4, 4), yh * 2 + other)

    def along_y(d):
        to = lax.rem(y + d, 8)
        return ((z * 2 + lax.rem(to, 2)) * 4 + x, (to // 2) * 2 + core)

    barrier = pltpu.get_barrier_semaphore()
    for d in range(1, 8):
        for peer in (along_z(d), along_xc(d), along_y(d)):
            pl.semaphore_signal(barrier, inc=1, device_id=peer, device_id_type=MESH)

    own = pltpu.make_async_copy(deltas.at[:, x], rx.at[:, x, pl.ds(0, ROWS)], own_sem)
    own.start()
    inputs = [
        pltpu.make_async_copy(here, there, in_sem.at[i])
        for i, (here, there) in enumerate(
            ((scales, scales_v), (master, master_v), (momentum, momentum_v), (clip, clip_v))
        )
    ]
    for copy in inputs:
        copy.start()
    pl.semaphore_wait(barrier, 21)

    def remote(src, dst, send, recv, to):
        copy = pltpu.make_async_remote_copy(
            src_ref=src, dst_ref=dst, send_sem=send, recv_sem=recv, device_id=to, device_id_type=MESH
        )
        copy.start()
        return copy

    def chunk(mine, dz):
        return 2 * lax.rem(z + dz, 8) + (yl if mine else 1 - yl)

    xcopies = []
    for s, (mine, dz) in enumerate(SEQUENCE):
        zy = chunk(mine, dz)
        xcopies.append(
            [
                remote(
                    deltas.at[zy, lax.rem(x + d, 4)], rx.at[zy, x, pl.ds(0, ROWS)],
                    xs.at[s, k], xr.at[s, k], along_x(d),
                )
                for k, d in enumerate((2, 1, 3))
            ]
        )
        if s == 1:
            inputs[0].wait()
            flat = scales_v[...].astype(F32)
            for r in range(NX * NY * NZ):
                table[r % 4, r // 4 : r // 4 + 1, 0:ROWS] = flat[:, ROWS * r : ROWS * (r + 1)]
            for k in range(4):
                table16[k] = table[k].astype(BF16)
            scopies = [
                remote(table16.at[lax.rem(x + d, 4)], rs.at[x], ss.at[k], sr.at[k], along_x(d))
                for k, d in enumerate((2, 1, 3))
            ]

    def spread(blocks, send, recv):
        copies = []
        for i, d in enumerate((1, 7, 2, 6)):
            copies.append(remote(blocks.at[z], blocks.at[z], send.at[i], recv.at[i], along_z(d)))
        return copies

    def pass_on(blocks, send, recv, copies):
        for i, d in ((2, 2), (3, 6)):
            copies[i].wait()
            source = lax.rem(z + 8 - d, 8)
            block = blocks.at[source]
            copies.append(remote(block, block, send.at[i + 2], recv.at[i + 2], along_z(1 if d == 2 else 7)))
            half = blocks.at[source, pl.ds(0 if d == 2 else ROWS // 2, ROWS // 2)]
            copies.append(remote(half, half, send.at[i + 4], recv.at[i + 4], along_z(d)))
        return copies[:2] + copies[4:]

    inputs[1].wait()
    inputs[2].wait()
    az[z] = master_v[...] - 0.567 * momentum_v[...]
    acopies = spread(az, as_, ar)

    for zy in range(16):
        for k in range(4):
            rx[zy, k, ROWS:PAD] = jnp.zeros((PAD - ROWS, 128), BF16)
    for copy in scopies:
        copy.wait()
    for k in range(4):
        sf[k] = rs[k].astype(F32)
    sf[x] = table[x]
    own.wait()

    eye = lax.broadcasted_iota(jnp.int32, (ROWS, PAD), 0) == lax.broadcasted_iota(jnp.int32, (ROWS, PAD), 1)

    def decode(zy):
        diags = [
            jnp.where(eye, jnp.broadcast_to(sf[k, pl.ds(zy, 1), :], (ROWS, PAD)), 0.0).astype(BF16)
            for k in range(4)
        ]
        return jnp.dot(
            jnp.concatenate(diags, axis=1), rx[zy].reshape(4 * PAD, 128), preferred_element_type=F32
        )

    ycopies, zcopies = {}, []
    for s, (mine, dz) in enumerate(SEQUENCE):
        for copy in xcopies[s]:
            copy.wait()
        part = decode(chunk(mine, dz))
        if not mine:
            ysrc[dz] = part
            ycopies[dz] = remote(ysrc.at[dz], yrx.at[dz], ys.at[dz], yr.at[dz], y_peer)
        else:
            ycopies[dz].wait()
            total = part + yrx[dz]
            if dz:
                zsrc[dz - 1] = total
                zcopies.append(
                    remote(zsrc.at[dz - 1], zrx.at[dz - 1], zs.at[dz - 1], zr.at[dz - 1], along_z(dz))
                )
        if s == 5:
            acopies = pass_on(az, as_, ar, acopies)
    for copy in zcopies:
        copy.wait()
    for i in range(7):
        total = total + zrx[i]
    grad = total * (1.0 / (NX * NY * NZ))
    gz[z] = grad
    partial = jnp.sum((grad * grad).reshape(ROWS // 8, 8, 128), axis=0)
    sq[0] = partial
    for stage, way in enumerate((along_z, along_y, along_xc)):
        copies = [
            remote(sq.at[stage], ar_rx.at[stage, d - 1], qs.at[stage, d - 1], qr.at[stage, d - 1], way(d))
            for d in (4, 3, 5, 2, 6, 1, 7)
        ]
        if stage == 0:
            gcopies = spread(gz, gs, gr)
            grad_out[...] = grad
        elif stage == 1:
            gcopies = pass_on(gz, gs, gr, gcopies)
        for copy in copies:
            copy.wait()
        for d in range(7):
            partial = partial + ar_rx[stage, d]
        if stage == 0:
            sq[1] = partial
        elif stage == 1:
            sq[2] = partial
    mean = jnp.sum(jnp.sum(partial, axis=1, keepdims=True), axis=0, keepdims=True) * (1.0 / (512 * ROWS * 128))
    inputs[3].wait()
    factor = jnp.minimum(1.0, clip_v[...] / jnp.sqrt(mean + 1e-06))
    factor_out[...] = jnp.broadcast_to(factor, (8, 128))
    for copy in acopies + gcopies:
        copy.wait()
    step = 1.33 * factor

    counter = [0]

    def base_to(zi, yy, xx, to, src=None):
        n = counter[0]
        counter[0] += 1
        block = gathered.at[zi, yy, xx]
        return remote(block if src is None else src, block, bs.at[n], br.at[n], to)

    right, left = along_x(1), along_x(3)
    x_left, x_right = lax.rem(x + 3, 4), lax.rem(x + 1, 4)
    x_far = lax.rem(x + 2, 4)
    done, a_x, b_y = [], {}, {}
    for i in range(4):
        for zi in (i, i + 4):
            nb[zi] = (az[zi] - step * gz[zi]).astype(BF16)
        b_y[i + 4] = base_to(i + 4, yl, x, y_peer, nb.at[i + 4])
        a_x[i] = (
            base_to(i, yl, x, right, nb.at[i]), base_to(i, yl, x, left, nb.at[i]),
        )
    whole = pltpu.make_async_copy(nb, gathered.at[:, yl, x], own_sem)
    whole.start()
    b_x, b_x2, a_far, b_far = {}, {}, {}, {}
    for i in range(4):
        done.append(base_to(i, yl, x, y_peer, nb.at[i]))
        zi = i + 4
        b_x[zi] = (base_to(zi, yl, x, right, nb.at[zi]), base_to(zi, yl, x, left, nb.at[zi]))
    for i in range(4):
        from_left, from_right = a_x[i]
        from_left.wait()
        from_right.wait()
        if i % 2 == 0:
            a_far[i] = base_to(i, yl, x_left, right)
        else:
            a_far[i] = base_to(i, yl, x_right, left)
        done.append(base_to(i, yl, x_left, y_peer))
        done.append(base_to(i, yl, x_right, y_peer))
        zi = i + 4
        b_y[zi].wait()
        b_x2[zi] = (base_to(zi, 1 - yl, x, right), base_to(zi, 1 - yl, x, left))
    for i in range(4):
        a_far[i].wait()
        done.append(base_to(i, yl, x_far, y_peer))
        zi = i + 4
        for yy, pair in ((yl, b_x[zi]), (1 - yl, b_x2[zi])):
            for copy in pair:
                copy.wait()
            if i % 2 == 0:
                done.append(base_to(zi, yy, x_left, right))
            else:
                done.append(base_to(zi, yy, x_right, left))
    whole.wait()
    for copy in done:
        copy.wait()


def finish_kernel(
    gathered, grad, factor, master, momentum,
    base, new_master, new_momentum,
    blocks, rows, grad_v, factor_v, master_v, momentum_v, nm_v, nmom_v, in_sem, small_sem, out_sem,
):
    ins = [
        pltpu.make_async_copy(gathered.at[pl.ds(16 * i, 16), h], blocks.at[i, h], in_sem.at[i, h])
        for i in range(2) for h in range(2)
    ]
    smalls = [
        pltpu.make_async_copy(here, there, small_sem.at[i])
        for i, (here, there) in enumerate(
            ((grad, grad_v), (factor, factor_v), (master, master_v), (momentum, momentum_v))
        )
    ]
    for copy in smalls + ins:
        copy.start()
    for copy in smalls:
        copy.wait()
    scaled = factor_v[0:1, 0:1] * grad_v[...]
    moved = 0.9 * momentum_v[...] + scaled
    nmom_v[...] = moved
    nm_v[...] = master_v[...] - 0.7 * (scaled + 0.9 * moved)
    outs = [
        pltpu.make_async_copy(nm_v, new_master, out_sem.at[4]),
        pltpu.make_async_copy(nmom_v, new_momentum, out_sem.at[5]),
    ]
    for copy in outs:
        copy.start()
    for n in range(4):
        i, h = n // 2, n % 2
        ins[n].wait()
        for j in range(0, ROWS, 16):
            turned = jnp.swapaxes(blocks[i, h, :, j : j + 16, :], 0, 1)
            for k in range(16):
                rows[i, h, :, 128 * (j + k) : 128 * (j + k + 1)] = turned[k]
        out = pltpu.make_async_copy(
            rows.at[i, h], base.at[pl.ds(16 * i, 16), pl.ds(h * (FF // 2), FF // 2)], out_sem.at[n]
        )
        out.start()
        outs.append(out)
    for copy in outs:
        copy.wait()


def per_device(deltas, scales, clip_level, master, momentum):
    vmem, anywhere = pl.BlockSpec(memory_space=pltpu.VMEM), pl.BlockSpec(memory_space=pl.ANY)
    dma = pltpu.SemaphoreType.DMA
    gathered, grad, factor = pl.pallas_call(
        kernel,
        out_shape=(
            jax.ShapeDtypeStruct((NZ, NY, NX, ROWS, 128), BF16),
            jax.ShapeDtypeStruct((ROWS, 128), F32),
            jax.ShapeDtypeStruct((8, 128), F32),
        ),
        in_specs=[anywhere] * 5,
        out_specs=(anywhere, vmem, vmem),
        scratch_shapes=[
            pltpu.VMEM((1, NZ * NY * NX * ROWS), BF16),
            pltpu.VMEM((1, 1), F32),
            pltpu.VMEM((ROWS, 128), F32),
            pltpu.VMEM((ROWS, 128), F32),
            pltpu.VMEM((NZ * NY, NX, PAD, 128), BF16),
            pltpu.VMEM((NX, NZ * NY, 128), F32),
            pltpu.VMEM((NX, NZ * NY, 128), BF16),
            pltpu.VMEM((NX, NZ * NY, 128), BF16),
            pltpu.VMEM((NX, NZ * NY, 128), F32),
            pltpu.VMEM((NZ, ROWS, 128), F32),
            pltpu.VMEM((NZ, ROWS, 128), F32),
            pltpu.VMEM((NZ - 1, ROWS, 128), F32),
            pltpu.VMEM((NZ - 1, ROWS, 128), F32),
            pltpu.VMEM((NZ, ROWS, 128), F32),
            pltpu.VMEM((NZ, ROWS, 128), F32),
            pltpu.VMEM((NZ, ROWS, 128), BF16),
            pltpu.VMEM((3, 8, 128), F32),
            pltpu.VMEM((3, 7, 8, 128), F32),
            dma,
            dma((4,)),
            dma((16, 3)), dma((16, 3)),
            dma((3,)), dma((3,)),
            dma((8,)), dma((8,)),
            dma((7,)), dma((7,)),
            dma((8,)), dma((8,)),
            dma((8,)), dma((8,)),
            dma((3, 7)), dma((3, 7)),
            dma((56,)), dma((56,)),
        ],
        compiler_params=pltpu.CompilerParams(
            collective_id=0, has_side_effects=True, vmem_limit_bytes=60 * 2**20
        ),
    )(
        deltas.reshape(NZ * NY, NX, ROWS, 128), scales, clip_level.reshape(1, 1), master, momentum
    )
    half = FF // 2
    return pl.pallas_call(
        finish_kernel,
        out_shape=(
            jax.ShapeDtypeStruct((32, FF), BF16),
            jax.ShapeDtypeStruct((ROWS, 128), F32),
            jax.ShapeDtypeStruct((ROWS, 128), F32),
        ),
        in_specs=[anywhere] * 5,
        out_specs=(anywhere,) * 3,
        scratch_shapes=[
            pltpu.VMEM((2, 2, 16, ROWS, 128), BF16),
            pltpu.VMEM((2, 2, 16, half), BF16),
            pltpu.VMEM((ROWS, 128), F32),
            pltpu.VMEM((8, 128), F32),
            pltpu.VMEM((ROWS, 128), F32),
            pltpu.VMEM((ROWS, 128), F32),
            pltpu.VMEM((ROWS, 128), F32),
            pltpu.VMEM((ROWS, 128), F32),
            dma((2, 2)), dma((4,)), dma((6,)),
        ],
        compiler_params=pltpu.CompilerParams(vmem_limit_bytes=60 * 2**20),
    )(gathered.reshape(32, 2, ROWS, 128), grad, factor, master, momentum)


def solution(mesh):
    fr = ("fsdp", "rep")
    in_specs = (P("rep", "fsdp", None), P("rep", "fsdp"), P(), P(fr, None), P(fr, None))
    out_specs = (P("fsdp", None), P(fr, None), P(fr, None))
    return jax.shard_map(
        per_device, mesh=mesh, in_specs=in_specs, out_specs=out_specs, check_vma=False
    )
```

time: 87.2 us -> 75.1 us (0.86); the launches traced: 85.5 us -> 75 us
  local copies, waits for them, and re-layouts: 6.31 us -> 0 us
  Pallas kernels: 77.9 us -> 73.7 us
    unnamed x14 -> x0, local copies, waits for them, and re-layouts: 6.31 us -> none
    pallas_call x1, Pallas kernels: 73.5 us -> 70.9 us  [per_device(): pl.pallas_call(kernel, out_shape=(jax.ShapeDtypeStruct((NZ, NY, NX, ROWS,...]
    pallas_call x1, Pallas kernels: 4.39 us -> 2.82 us  [per_device(): pl.pallas_call(finish_kernel, out_shape=(jax.ShapeDtypeStruct((32, FF), B...]
where the time goes in v2:
time: 75.1 us; the launch traced here: 75 us
  Pallas kernels  73.7 us (98%)
  between operations  1.28 us (2%)
    pallas_call x1, Pallas kernels, per_device(): pl.pallas_call(kernel, out_shape=(jax.ShapeDtypeStruct((NZ, NY, NX, ROWS,...  70.9 us
    pallas_call x1, Pallas kernels, per_device(): pl.pallas_call(finish_kernel, out_shape=(jax.ShapeDtypeStruct((32, FF), B...  2.82 us

profile of v2, /device:TPU:6, one launch (start us, length us, event | category | flops | bytes accessed | tf_op | source)
XLA Modules:
  0.0 75.0 jit_solution(2371898388942380521)
XLA Ops:
  1.3 70.9 %shard_map.76 = (bf16[8,2,4,112,128]{4,3,2,1,0:T(8,128)(2,1)}, f32[112,128]{1,0:T(8,128)}, f32[8,128]{1,0:T(8,128)}) custom-call(bf16[16,4,112,128]{3,2,1,0:T(8,128)(2,1)} %bitcast.4, bf16[1,7168]{1,0:T(2,128)(2,1)} %scales.1, f32[1,1]{1,0:T(1,128)} %bitcast.3.clip, f32[112,128]{1,0:T(8,128)} %master.3, f32[112,128]{1,0:T(8,128)} %momentum.3), custom_call_target="tpu_custom_call" | custom-call | tf_op jit(solution)/shard_map/pallas_call | solution.py:300
  72.2 2.8 %shard_map.77 = (bf16[32,28672]{1,0:T(8,128)(2,1)}, f32[112,128]{1,0:T(8,128)}, f32[112,128]{1,0:T(8,128)}) custom-call(bf16[32,2,112,128]{3,2,1,0:T(8,128)(2,1)} %bitcast.5, f32[112,128]{1,0:T(8,128)} %get-tuple-element.7.grad, f32[8,128]{1,0:T(8,128)} %get-tuple-element.8.factor, f32[112,128]{1,0:T(8,128)} %master.3, f32[112,128]{1,0:T(8,128)} %momentum.3), custom_call_target="tpu_custom_call" | custom-call | tf_op jit(solution)/shard_map/pallas_call | solution.py:346

commit v3 on v2

--- a/solution.py
+++ b/solution.py
@@ -13,8 +13,14 @@
 ROWS = 112
 PAD = 128
 SEQUENCE = (
-    (0, 4), (0, 3), (0, 5), (1, 4), (0, 2), (1, 3), (0, 6), (1, 5),
-    (0, 1), (0, 7), (0, 0), (1, 2), (1, 6), (1, 1), (1, 7), (1, 0),
+    (0, 4), (0, 3), (0, 5), (1, 4), (0, 2), (0, 6), (1, 3), (1, 5),
+    (0, 1), (1, 2), (0, 7), (1, 6), (0, 0), (1, 1), (1, 7), (1, 0),
+)
+ALONG_ZC = tuple((0, 0, d, c) for c in (1, 0) for d in (4, 3, 5, 2, 6, 1, 7, 0))[:-1]
+ALONG_YX = tuple((dx, d, 0, 0) for dx in (2, 1, 3, 0) for d in (4, 3, 5, 2, 6, 1, 7, 0))[:-1]
+GREETED = (
+    (1, 0, 0, 0), (2, 0, 0, 0), (3, 0, 0, 0), (0, 0, 0, 1), (0, 0, 1, 0), (0, 0, 2, 0), (0, 0, 6, 0), (0, 0, 7, 0),
+    (0, 1, 0, 0), (0, 2, 0, 0), (0, 6, 0, 0), (0, 7, 0, 0),
 )
 BF16, F32 = jnp.bfloat16, jnp.float32
 
@@ -23,7 +29,7 @@
     deltas, scales, clip, master, momentum,
     gathered, grad_out, factor_out,
     scales_v, clip_v, master_v, momentum_v, rx, table, table16, rs, sf, ysrc, yrx, zsrc, zrx, az, gz, nb, sq, ar_rx,
-    own_sem, in_sem, xs, xr, ss, sr, ys, yr, zs, zr, as_, ar, gs, gr, qs, qr, bs, br,
+    heard, own_sem, in_sem, xs, xr, ss, sr, ys, yr, zs, zr, as_, ar, gs, gr, qs, qr, bs, br,
 ):
     rep, fsdp = lax.axis_index("rep"), lax.axis_index("fsdp")
     x, yl, z = lax.rem(rep, 4), lax.rem(rep // 4, 2), rep // 8
@@ -41,18 +47,17 @@
 
     y_peer = device(x, 1 - yl, z)
 
-    def along_xc(d):
-        other = lax.rem(core + d // 4, 2)
-        return ((z * 2 + yl) * 4 + lax.rem(x + d % 4, 4), yh * 2 + other)
-
-    def along_y(d):
-        to = lax.rem(y + d, 8)
-        return ((z * 2 + lax.rem(to, 2)) * 4 + x, (to // 2) * 2 + core)
+    def partner(way):
+        dx, dy, dz, dc = way
+        to = lax.rem(y + dy, 8)
+        return (
+            (lax.rem(z + dz, 8) * 2 + lax.rem(to, 2)) * 4 + lax.rem(x + dx, 4),
+            (to // 2) * 2 + lax.rem(core + dc, 2),
+        )
 
     barrier = pltpu.get_barrier_semaphore()
-    for d in range(1, 8):
-        for peer in (along_z(d), along_xc(d), along_y(d)):
-            pl.semaphore_signal(barrier, inc=1, device_id=peer, device_id_type=MESH)
+    for way in GREETED:
+        pl.semaphore_signal(barrier, inc=1, device_id=partner(way), device_id_type=MESH)
 
     own = pltpu.make_async_copy(deltas.at[:, x], rx.at[:, x, pl.ds(0, ROWS)], own_sem)
     own.start()
@@ -64,7 +69,7 @@
     ]
     for copy in inputs:
         copy.start()
-    pl.semaphore_wait(barrier, 21)
+    pl.semaphore_wait(barrier, len(GREETED))
 
     def remote(src, dst, send, recv, to):
         copy = pltpu.make_async_remote_copy(
@@ -142,7 +147,7 @@
             jnp.concatenate(diags, axis=1), rx[zy].reshape(4 * PAD, 128), preferred_element_type=F32
         )
 
-    ycopies, zcopies = {}, []
+    ycopies, zcopies = {}, {}
     for s, (mine, dz) in enumerate(SEQUENCE):
         for copy in xcopies[s]:
             copy.wait()
@@ -153,40 +158,44 @@
         else:
             ycopies[dz].wait()
             total = part + yrx[dz]
+            before = {3: (4,), 2: (3,), 1: (2,), 6: (5,), 7: (6,), 0: (1, 7)}.get(dz, ())
+            for far in before:
+                zcopies[far].wait()
+                total = total + zrx[far - 1]
             if dz:
                 zsrc[dz - 1] = total
-                zcopies.append(
-                    remote(zsrc.at[dz - 1], zrx.at[dz - 1], zs.at[dz - 1], zr.at[dz - 1], along_z(dz))
+                zcopies[dz] = remote(
+                    zsrc.at[dz - 1], zrx.at[dz - 1], zs.at[dz - 1], zr.at[dz - 1], along_z(1 if dz < 5 else 7)
                 )
         if s == 5:
             acopies = pass_on(az, as_, ar, acopies)
-    for copy in zcopies:
-        copy.wait()
-    for i in range(7):
-        total = total + zrx[i]
+        if s in (2, 7):
+            if s == 7:
+                pl.semaphore_wait(heard.at[0], 4)
+            for d in (1, 2, 6, 7):
+                pl.semaphore_signal(
+                    heard.at[s // 7], inc=1, device_id=partner((0, d, 0, 0)), device_id_type=MESH
+                )
     grad = total * (1.0 / (NX * NY * NZ))
     gz[z] = grad
-    partial = jnp.sum((grad * grad).reshape(ROWS // 8, 8, 128), axis=0)
-    sq[0] = partial
-    for stage, way in enumerate((along_z, along_y, along_xc)):
+    pl.semaphore_wait(heard.at[1], 4)
+    partial = jnp.sum(grad * grad, axis=0, keepdims=True)
+    for stage, ways in enumerate((ALONG_ZC, ALONG_YX)):
+        first = stage * len(ALONG_ZC)
+        sq[stage] = partial
         copies = [
-            remote(sq.at[stage], ar_rx.at[stage, d - 1], qs.at[stage, d - 1], qr.at[stage, d - 1], way(d))
-            for d in (4, 3, 5, 2, 6, 1, 7)
+            remote(sq.at[stage], ar_rx.at[first + i], qs.at[first + i], qr.at[first + i], partner(way))
+            for i, way in enumerate(ways)
         ]
         if stage == 0:
             gcopies = spread(gz, gs, gr)
             grad_out[...] = grad
-        elif stage == 1:
+        else:
             gcopies = pass_on(gz, gs, gr, gcopies)
         for copy in copies:
             copy.wait()
-        for d in range(7):
-            partial = partial + ar_rx[stage, d]
-        if stage == 0:
-            sq[1] = partial
-        elif stage == 1:
-            sq[2] = partial
-    mean = jnp.sum(jnp.sum(partial, axis=1, keepdims=True), axis=0, keepdims=True) * (1.0 / (512 * ROWS * 128))
+        partial = partial + jnp.sum(ar_rx[first : first + len(ways)], axis=0)
+    mean = jnp.sum(partial, axis=1, keepdims=True) * (1.0 / (512 * ROWS * 128))
     inputs[3].wait()
     factor = jnp.minimum(1.0, clip_v[...] / jnp.sqrt(mean + 1e-06))
     factor_out[...] = jnp.broadcast_to(factor, (8, 128))
@@ -323,8 +332,9 @@
             pltpu.VMEM((NZ, ROWS, 128), F32),
             pltpu.VMEM((NZ, ROWS, 128), F32),
             pltpu.VMEM((NZ, ROWS, 128), BF16),
-            pltpu.VMEM((3, 8, 128), F32),
-            pltpu.VMEM((3, 7, 8, 128), F32),
+            pltpu.VMEM((2, 1, 128), F32),
+            pltpu.VMEM((46, 1, 128), F32),
+            pltpu.SemaphoreType.REGULAR((2,)),
             dma,
             dma((4,)),
             dma((16, 3)), dma((16, 3)),
@@ -333,7 +343,7 @@
             dma((7,)), dma((7,)),
             dma((8,)), dma((8,)),
             dma((8,)), dma((8,)),
-            dma((3, 7)), dma((3, 7)),
+            dma((46,)), dma((46,)),
             dma((56,)), dma((56,)),
         ],
         compiler_params=pltpu.CompilerParams(

time: 75.1 us -> 72.5 us (0.965)
  Pallas kernels: 73.7 us -> 71.1 us
    pallas_call x1, Pallas kernels: 70.9 us -> 68.3 us  [per_device(): pl.pallas_call(kernel, out_shape=(jax.ShapeDtypeStruct((NZ, NY, NX, ROWS,...]
where the time goes in v3:
time: 72.5 us; the launch traced here: 72.4 us
  Pallas kernels  71.1 us (98%)
  between operations  1.28 us (2%)
    pallas_call x1, Pallas kernels, per_device(): pl.pallas_call(kernel, out_shape=(jax.ShapeDtypeStruct((NZ, NY, NX, ROWS,...  68.3 us
    pallas_call x1, Pallas kernels, per_device(): pl.pallas_call(finish_kernel, out_shape=(jax.ShapeDtypeStruct((32, FF), B...  2.82 us

profile of v3, /device:TPU:6, one launch (start us, length us, event | category | flops | bytes accessed | tf_op | source)
XLA Modules:
  0.0 72.4 jit_solution(15354959170002366843)
XLA Ops:
  1.3 68.3 %shard_map.76 = (bf16[8,2,4,112,128]{4,3,2,1,0:T(8,128)(2,1)}, f32[112,128]{1,0:T(8,128)}, f32[8,128]{1,0:T(8,128)}) custom-call(bf16[16,4,112,128]{3,2,1,0:T(8,128)(2,1)} %bitcast.4, bf16[1,7168]{1,0:T(2,128)(2,1)} %scales.1, f32[1,1]{1,0:T(1,128)} %bitcast.3.clip, f32[112,128]{1,0:T(8,128)} %master.3, f32[112,128]{1,0:T(8,128)} %momentum.3), custom_call_target="tpu_custom_call" | custom-call | tf_op jit(solution)/shard_map/pallas_call | solution.py:309
  69.6 2.8 %shard_map.77 = (bf16[32,28672]{1,0:T(8,128)(2,1)}, f32[112,128]{1,0:T(8,128)}, f32[112,128]{1,0:T(8,128)}) custom-call(bf16[32,2,112,128]{3,2,1,0:T(8,128)(2,1)} %bitcast.5, f32[112,128]{1,0:T(8,128)} %get-tuple-element.7.grad, f32[8,128]{1,0:T(8,128)} %get-tuple-element.8.factor, f32[112,128]{1,0:T(8,128)} %master.3, f32[112,128]{1,0:T(8,128)} %momentum.3), custom_call_target="tpu_custom_call" | custom-call | tf_op jit(solution)/shard_map/pallas_call | solution.py:356

commit v4 on v3

v4 whole, which is shorter than its diff:
```python
import functools

import jax
import jax.numpy as jnp
from jax import lax
from jax.experimental import pallas as pl
from jax.experimental.pallas import tpu as pltpu
from jax.sharding import PartitionSpec as P

FF = 28672
MESH = pl.DeviceIdType.MESH
NX, NY, NZ = 4, 2, 8
ROWS = 112
PAD = 128
EARLY = 96
LATE = ROWS - EARLY
AHEAD = 6
SEQUENCE = (
    (0, 4), (0, 3), (0, 5), (1, 4), (0, 2), (0, 6), (1, 3), (1, 5),
    (0, 1), (1, 2), (0, 7), (1, 6), (0, 0), (1, 1), (1, 7), (1, 0),
)
ALONG_ZC = tuple((0, 0, d, c) for c in (1, 0) for d in (4, 3, 5, 2, 6, 1, 7, 0))[:-1]
ALONG_YX = tuple((dx, d, 0, 0) for dx in (2, 1, 3, 0) for d in (4, 3, 5, 2, 6, 1, 7, 0))[:-1]
GREETED = (
    (1, 0, 0, 0), (2, 0, 0, 0), (3, 0, 0, 0), (0, 0, 0, 1), (0, 0, 1, 0), (0, 0, 2, 0), (0, 0, 6, 0), (0, 0, 7, 0),
    (0, 1, 0, 0), (0, 2, 0, 0), (0, 6, 0, 0), (0, 7, 0, 0),
)
BF16, F32 = jnp.bfloat16, jnp.float32


def kernel(
    deltas, scales, clip, master, momentum,
    gathered, grad_out, factor_out,
    scales_v, clip_v, master_v, momentum_v, rx, table, table16, rs, sf, ysrc, yrx, zsrc, zrx, az, gz, nb, cx, nbc, rxl, tl, rl, ylsrc, ylrx, xlsrc, xlrx, sq, ar_rx,
    heard, own_sem, late_sem, in_sem, xs, xr, ss, sr, ys, yr, zs, zr, as_, ar, gs, gr, cs, cr, qs, qr, bs, br, ds_, dr, zls, zlr, tls, tlr, yls, ylr, xls, xlr,
):
    rep, fsdp = lax.axis_index("rep"), lax.axis_index("fsdp")
    x, yl, z = lax.rem(rep, 4), lax.rem(rep // 4, 2), rep // 8
    yh, core = fsdp // 2, lax.rem(fsdp, 2)
    y = yh * 2 + yl

    def device(x, yl, z):
        return ((z * 2 + yl) * 4 + x, fsdp)

    def along_x(d):
        return device(lax.rem(x + d, 4), yl, z)

    def along_z(d):
        return device(x, yl, lax.rem(z + d, 8))

    y_peer = device(x, 1 - yl, z)

    def partner(way):
        dx, dy, dz, dc = way
        to = lax.rem(y + dy, 8)
        return (
            (lax.rem(z + dz, 8) * 2 + lax.rem(to, 2)) * 4 + lax.rem(x + dx, 4),
            (to // 2) * 2 + lax.rem(core + dc, 2),
        )

    barrier = pltpu.get_barrier_semaphore()
    for way in GREETED:
        pl.semaphore_signal(barrier, inc=1, device_id=partner(way), device_id_type=MESH)

    own = pltpu.make_async_copy(deltas.at[:, x, pl.ds(0, EARLY)], rx.at[:, x, pl.ds(0, EARLY)], own_sem)
    own.start()
    late_here = rxl.at[:, :, pl.ds(pl.multiple_of(LATE * z, LATE), LATE)]
    own_late = pltpu.make_async_copy(deltas.at[pl.ds(2 * z, 2), :, pl.ds(EARLY, LATE)], late_here, late_sem)
    own_late.start()
    inputs = [
        pltpu.make_async_copy(here, there, in_sem.at[i])
        for i, (here, there) in enumerate(
            ((scales, scales_v), (master, master_v), (momentum, momentum_v), (clip, clip_v))
        )
    ]
    for copy in inputs:
        copy.start()
    pl.semaphore_wait(barrier, len(GREETED))

    def remote(src, dst, send, recv, to):
        copy = pltpu.make_async_remote_copy(
            src_ref=src, dst_ref=dst, send_sem=send, recv_sem=recv, device_id=to, device_id_type=MESH
        )
        copy.start()
        return copy

    def chunk(mine, dz):
        return 2 * lax.rem(z + dz, 8) + (yl if mine else 1 - yl)

    def send_along_x(s):
        zy = chunk(*SEQUENCE[s])
        return [
            remote(
                deltas.at[zy, lax.rem(x + d, 4), pl.ds(0, EARLY)], rx.at[zy, x, pl.ds(0, EARLY)],
                xs.at[s, k], xr.at[s, k], along_x(d),
            )
            for k, d in enumerate((2, 1, 3))
        ]

    xcopies = [send_along_x(0), send_along_x(1)]
    for d in (1, 2, 6, 7):
        for way in ((0, d, 0, 0), (0, 0, d, 0)):
            pl.semaphore_signal(heard.at[0], inc=1, device_id=partner(way), device_id_type=MESH)
    inputs[0].wait()
    flat = scales_v[...].astype(F32)
    for r in range(NX * NY * NZ):
        table[r % 4, r // 4 : r // 4 + 1, 0:ROWS] = flat[:, ROWS * r : ROWS * (r + 1)]
    for k in range(4):
        table16[k] = table[k].astype(BF16)
    scopies = [
        remote(table16.at[lax.rem(x + d, 4)], rs.at[x], ss.at[k], sr.at[k], along_x(d))
        for k, d in enumerate((2, 1, 3))
    ]
    for s in range(2, AHEAD):
        xcopies.append(send_along_x(s))
    lanes = lax.broadcasted_iota(jnp.int32, (NZ * NY, 128), 1) // LATE == z
    for k in range(4):
        values = jnp.concatenate([table[k][:, EARLY:ROWS]] * 8, axis=1)
        values = jnp.where(lanes, values, 0.0)
        for zy in range(16):
            tl[zy // 2, 4 * (zy % 2) + k : 4 * (zy % 2) + k + 1, :] = values[zy : zy + 1]
    pl.semaphore_wait(heard.at[0], 8)
    lcopies = []
    for i, d in enumerate((4, 3, 5, 2, 6, 1, 7)):
        to = lax.rem(z + d, 8)
        lcopies.append(remote(tl.at[to], rl.at[z], tls.at[i], tlr.at[i], along_z(d)))
        lcopies.append(
            remote(
                deltas.at[pl.ds(2 * to, 2), :, pl.ds(EARLY, LATE)], late_here, zls.at[i], zlr.at[i], along_z(d)
            )
        )

    def spread(blocks, send, recv):
        copies = []
        for i, d in enumerate((1, 7, 2, 6)):
            copies.append(remote(blocks.at[z], blocks.at[z], send.at[i], recv.at[i], along_z(d)))
        return copies

    def pass_on(blocks, send, recv, copies):
        for i, d in ((2, 2), (3, 6)):
            copies[i].wait()
            source = lax.rem(z + 8 - d, 8)
            block = blocks.at[source]
            copies.append(remote(block, block, send.at[i + 2], recv.at[i + 2], along_z(1 if d == 2 else 7)))
            half = blocks.at[source, pl.ds(0 if d == 2 else EARLY // 2, EARLY // 2)]
            copies.append(remote(half, half, send.at[i + 4], recv.at[i + 4], along_z(d)))
        return copies[:2] + copies[4:]

    inputs[1].wait()
    inputs[2].wait()
    moved = master_v[...] - 0.567 * momentum_v[...]
    az[z] = moved[:EARLY]
    cx[yl, x, 0] = moved[EARLY:]

    for zy in range(16):
        for k in range(4):
            rx[zy, k, EARLY:PAD] = jnp.zeros((PAD - EARLY, 128), BF16)
    for copy in scopies:
        copy.wait()
    for k in range(4):
        sf[k] = rs[k].astype(F32)
    sf[x] = table[x]
    own.wait()

    eye = lax.broadcasted_iota(jnp.int32, (EARLY, PAD), 0) == lax.broadcasted_iota(jnp.int32, (EARLY, PAD), 1)

    def decode(zy):
        diags = [
            jnp.where(eye, jnp.broadcast_to(sf[k, pl.ds(zy, 1), :], (EARLY, PAD)), 0.0).astype(BF16)
            for k in range(4)
        ]
        return jnp.dot(
            jnp.concatenate(diags, axis=1), rx[zy].reshape(4 * PAD, 128), preferred_element_type=F32
        )

    late_eye = lax.rem(lax.broadcasted_iota(jnp.int32, (LATE, 128), 1), LATE) == lax.broadcasted_iota(
        jnp.int32, (LATE, 128), 0
    )

    def decode_late(yy, xx, late_scales):
        row = 4 * yy + xx
        diag = jnp.where(late_eye, jnp.broadcast_to(late_scales[pl.ds(row, 1), :], (LATE, 128)), 0.0)
        return jnp.dot(diag.astype(BF16), rxl[yy, xx], preferred_element_type=F32)

    ycopies, zcopies = {}, {}
    for s, (mine, dz) in enumerate(SEQUENCE):
        for copy in xcopies[s]:
            copy.wait()
        if s + AHEAD < len(SEQUENCE):
            xcopies.append(send_along_x(s + AHEAD))
        part = decode(chunk(mine, dz))
        if not mine:
            ysrc[dz] = part
            ycopies[dz] = remote(ysrc.at[dz], yrx.at[dz], ys.at[dz], yr.at[dz], y_peer)
        else:
            ycopies[dz].wait()
            total = part + yrx[dz]
            before = {3: (4,), 2: (3,), 1: (2,), 6: (5,), 7: (6,), 0: (1, 7)}.get(dz, ())
            for far in before:
                zcopies[far].wait()
                total = total + zrx[far - 1]
            if dz:
                zsrc[dz - 1] = total
                zcopies[dz] = remote(
                    zsrc.at[dz - 1], zrx.at[dz - 1], zs.at[dz - 1], zr.at[dz - 1], along_z(1 if dz < 5 else 7)
                )
        if s == 8:
            acopies = spread(az, as_, ar)
        if s == 7:
            for d in (1, 2, 6, 7):
                pl.semaphore_signal(
                    heard.at[1], inc=1, device_id=partner((0, d, 0, 0)), device_id_type=MESH
                )
        if s == 9:
            own_late.wait()
            for copy in lcopies:
                copy.wait()
            rl[z] = tl[z]
            tl[0] = jnp.sum(rl[...], axis=0)
            for xx in range(4):
                ylsrc[xx] = decode_late(1 - yl, xx, tl.at[0])
            ylcopy = remote(ylsrc, ylrx, yls, ylr, y_peer)
            for xx in range(4):
                xlsrc[xx] = decode_late(yl, xx, tl.at[0])
        if s == 12:
            ylcopy.wait()
            for xx in range(4):
                xlsrc[xx] = xlsrc[xx] + ylrx[xx]
            xlcopies = [
                remote(xlsrc.at[lax.rem(x + d, 4)], xlrx.at[k], xls.at[k], xlr.at[k], along_x(d))
                for k, d in enumerate((2, 1, 3))
            ]
    late_total = xlsrc[x]
    for k, copy in enumerate(xlcopies):
        copy.wait()
        late_total = late_total + xlrx[k]
    total = jnp.concatenate([total, late_total], axis=0)
    grad = total * (1.0 / (NX * NY * NZ))
    gz[z] = grad[:EARLY]
    cx[yl, x, 1] = grad[EARLY:]
    pl.semaphore_wait(heard.at[1], 4)
    partial = jnp.sum(grad * grad, axis=0, keepdims=True)
    for stage, ways in enumerate((ALONG_ZC, ALONG_YX)):
        first = stage * len(ALONG_ZC)
        sq[stage] = partial
        copies = [
            remote(sq.at[stage], ar_rx.at[first + i], qs.at[first + i], qr.at[first + i], partner(way))
            for i, way in enumerate(ways)
        ]
        if stage == 0:
            gcopies = spread(gz, gs, gr)
            acopies = pass_on(az, as_, ar, acopies)
            late = [
                remote(
                    cx.at[yl, x], cx.at[yl, x], cs.at[i], cr.at[i],
                    device(lax.rem(x + d, 4), (1 - yl) if other else yl, z),
                )
                for i, (other, d) in enumerate(((1, 2), (1, 1), (1, 3), (1, 0), (0, 2), (0, 1), (0, 3)))
            ]
            grad_out[...] = grad
        else:
            gcopies = pass_on(gz, gs, gr, gcopies)
        for copy in copies:
            copy.wait()
        partial = partial + jnp.sum(ar_rx[first : first + len(ways)], axis=0)
    mean = jnp.sum(partial, axis=1, keepdims=True) * (1.0 / (512 * ROWS * 128))
    inputs[3].wait()
    factor = jnp.minimum(1.0, clip_v[...] / jnp.sqrt(mean + 1e-06))
    factor_out[...] = jnp.broadcast_to(factor, (8, 128))
    step = 1.33 * factor
    for copy in late:
        copy.wait()
    for yy in range(NY):
        for xx in range(NX):
            nbc[yy, xx] = (cx[yy, xx, 0] - step * cx[yy, xx, 1]).astype(BF16)
    here = gathered.at[z, :, :, pl.ds(EARLY, LATE)]
    done = [
        remote(nbc, here, ds_.at[i], dr.at[i], along_z(d)) for i, d in enumerate((4, 3, 5, 2, 6, 1, 7))
    ]
    late_own = pltpu.make_async_copy(nbc, here, late_sem)
    late_own.start()
    for copy in acopies + gcopies:
        copy.wait()

    half = EARLY // 2
    items_a = ((0, 0, EARLY), (1, 0, EARLY), (2, 0, EARLY), (3, 0, half))
    items_b = ((4, 0, EARLY), (5, 0, EARLY), (6, 0, EARLY), (3, half, half), (7, 0, EARLY))
    counter = [0]

    def base_to(item, yy, xx, to, first=False):
        n = counter[0]
        counter[0] += 1
        zi, row, rows = item
        block = gathered.at[zi, yy, xx, pl.ds(row, rows)]
        return remote(nb.at[zi, pl.ds(row, rows)] if first else block, block, bs.at[n], br.at[n], to)

    right, left = along_x(1), along_x(3)
    x_left, x_right = lax.rem(x + 3, 4), lax.rem(x + 1, 4)
    x_far = lax.rem(x + 2, 4)

    def both_ways(item, yy, first=False):
        return base_to(item, yy, x, right, first), base_to(item, yy, x, left, first)

    def further(item, yy, way):
        return base_to(item, yy, x_left, right) if way else base_to(item, yy, x_right, left)

    a_x, b_y = [], []
    for i in range(5):
        for zi in ((0, 4), (1, 5), (2, 6), (3,), (7,))[i]:
            nb[zi] = (az[zi] - step * gz[zi]).astype(BF16)
        b_y.append(base_to(items_b[i], yl, x, y_peer, True))
        if i < 4:
            a_x.append(both_ways(items_a[i], yl, True))
    whole = pltpu.make_async_copy(nb, gathered.at[:, yl, x, pl.ds(0, EARLY)], own_sem)
    whole.start()
    b_x, b_x2, a_far = [], [], []
    for i in range(5):
        if i < 4:
            done.append(base_to(items_a[i], yl, x, y_peer, True))
        b_x.append(both_ways(items_b[i], yl, True))
    for i in range(5):
        if i < 4:
            for copy in a_x[i]:
                copy.wait()
            a_far.append(further(items_a[i], yl, i % 2 == 0))
            done.append(base_to(items_a[i], yl, x_left, y_peer))
            done.append(base_to(items_a[i], yl, x_right, y_peer))
        b_y[i].wait()
        b_x2.append(both_ways(items_b[i], 1 - yl))
    for i in range(5):
        if i < 4:
            a_far[i].wait()
            done.append(base_to(items_a[i], yl, x_far, y_peer))
        for yy, pair, way in ((yl, b_x[i], i % 2 == 1), (1 - yl, b_x2[i], i % 2 == 0)):
            for copy in pair:
                copy.wait()
            done.append(further(items_b[i], yy, way))
    late_own.wait()
    whole.wait()
    for copy in done:
        copy.wait()


def finish_kernel(
    gathered, grad, factor, master, momentum,
    base, new_master, new_momentum,
    rows, master_v, momentum_v, nm_v, nmom_v, small_sem, out_sem,
):
    smalls = [
        pltpu.make_async_copy(here, there, small_sem.at[i])
        for i, (here, there) in enumerate(
            ((master, master_v), (momentum, momentum_v))
        )
    ]
    for copy in smalls:
        copy.start()
    outs = []
    for n in range(4):
        i, h = n // 2, n % 2
        for j in range(0, ROWS, 16):
            turned = jnp.swapaxes(gathered[16 * i : 16 * (i + 1), h, j : j + 16, :], 0, 1)
            for k in range(16):
                rows[i, h, :, 128 * (j + k) : 128 * (j + k + 1)] = turned[k]
        out = pltpu.make_async_copy(
            rows.at[i, h], base.at[pl.ds(16 * i, 16), pl.ds(h * (FF // 2), FF // 2)], out_sem.at[n]
        )
        out.start()
        outs.append(out)
    for copy in smalls:
        copy.wait()
    scaled = factor[0:1, 0:1] * grad[...]
    moved = 0.9 * momentum_v[...] + scaled
    nmom_v[...] = moved
    nm_v[...] = master_v[...] - 0.7 * (scaled + 0.9 * moved)
    outs += [
        pltpu.make_async_copy(nm_v, new_master, out_sem.at[4]),
        pltpu.make_async_copy(nmom_v, new_momentum, out_sem.at[5]),
    ]
    for copy in outs[4:]:
        copy.start()
    for copy in outs:
        copy.wait()


def per_device(deltas, scales, clip_level, master, momentum):
    vmem, anywhere = pl.BlockSpec(memory_space=pltpu.VMEM), pl.BlockSpec(memory_space=pl.ANY)
    dma = pltpu.SemaphoreType.DMA
    deltas, scales, master, momentum = (
        pltpu.with_memory_space_constraint(a, pltpu.HBM)
        for a in (deltas.reshape(NZ * NY, NX, ROWS, 128), scales, master, momentum)
    )
    gathered, grad, factor = pl.pallas_call(
        kernel,
        out_shape=(
            pltpu.VMEM((NZ, NY, NX, ROWS, 128), BF16),
            pltpu.VMEM((ROWS, 128), F32),
            pltpu.VMEM((8, 128), F32),
        ),
        in_specs=[anywhere] * 5,
        out_specs=(vmem, vmem, vmem),
        scratch_shapes=[
            pltpu.VMEM((1, NZ * NY * NX * ROWS), BF16),
            pltpu.VMEM((1, 1), F32),
            pltpu.VMEM((ROWS, 128), F32),
            pltpu.VMEM((ROWS, 128), F32),
            pltpu.VMEM((NZ * NY, NX, PAD, 128), BF16),
            pltpu.VMEM((NX, NZ * NY, 128), F32),
            pltpu.VMEM((NX, NZ * NY, 128), BF16),
            pltpu.VMEM((NX, NZ * NY, 128), BF16),
            pltpu.VMEM((NX, NZ * NY, 128), F32),
            pltpu.VMEM((NZ, EARLY, 128), F32),
            pltpu.VMEM((NZ, EARLY, 128), F32),
            pltpu.VMEM((NZ - 1, EARLY, 128), F32),
            pltpu.VMEM((NZ - 1, EARLY, 128), F32),
            pltpu.VMEM((NZ, EARLY, 128), F32),
            pltpu.VMEM((NZ, EARLY, 128), F32),
            pltpu.VMEM((NZ, EARLY, 128), BF16),
            pltpu.VMEM((NY, NX, 2, LATE, 128), F32),
            pltpu.VMEM((NY, NX, LATE, 128), BF16),
            pltpu.VMEM((NY, NX, NZ * LATE, 128), BF16),
            pltpu.VMEM((NZ, NY * NX, 128), F32),
            pltpu.VMEM((NZ, NY * NX, 128), F32),
            pltpu.VMEM((NX, LATE, 128), F32),
            pltpu.VMEM((NX, LATE, 128), F32),
            pltpu.VMEM((NX, LATE, 128), F32),
            pltpu.VMEM((NX - 1, LATE, 128), F32),
            pltpu.VMEM((2, 1, 128), F32),
            pltpu.VMEM((46, 1, 128), F32),
            pltpu.SemaphoreType.REGULAR((2,)),
            dma,
            dma,
            dma((4,)),
            dma((16, 3)), dma((16, 3)),
            dma((3,)), dma((3,)),
            dma((8,)), dma((8,)),
            dma((7,)), dma((7,)),
            dma((8,)), dma((8,)),
            dma((8,)), dma((8,)),
            dma((7,)), dma((7,)),
            dma((46,)), dma((46,)),
            dma((63,)), dma((63,)),
            dma((7,)), dma((7,)),
            dma((7,)), dma((7,)),
            dma((7,)), dma((7,)),
            dma, dma,
            dma((3,)), dma((3,)),
        ],
        compiler_params=pltpu.CompilerParams(
            collective_id=0, has_side_effects=True, vmem_limit_bytes=40 * 2**20
        ),
    )(
        deltas, scales, clip_level.reshape(1, 1), master, momentum
    )
    half = FF // 2
    return pl.pallas_call(
        finish_kernel,
        out_shape=(
            jax.ShapeDtypeStruct((32, FF), BF16),
            jax.ShapeDtypeStruct((ROWS, 128), F32),
            jax.ShapeDtypeStruct((ROWS, 128), F32),
        ),
        in_specs=[vmem] * 3 + [anywhere] * 2,
        out_specs=(anywhere,) * 3,
        scratch_shapes=[
            pltpu.VMEM((2, 2, 16, half), BF16),
            pltpu.VMEM((ROWS, 128), F32),
            pltpu.VMEM((ROWS, 128), F32),
            pltpu.VMEM((ROWS, 128), F32),
            pltpu.VMEM((ROWS, 128), F32),
            dma((2,)), dma((6,)),
        ],
        compiler_params=pltpu.CompilerParams(vmem_limit_bytes=40 * 2**20),
    )(gathered.reshape(32, 2, ROWS, 128), grad, factor, master, momentum)


def solution(mesh):
    fr = ("fsdp", "rep")
    in_specs = (P("rep", "fsdp", None), P("rep", "fsdp"), P(), P(fr, None), P(fr, None))
    out_specs = (P("fsdp", None), P(fr, None), P(fr, None))
    return jax.shard_map(
        per_device, mesh=mesh, in_specs=in_specs, out_specs=out_specs, check_vma=False
    )
```

time: 72.5 us -> 69.4 us (0.957); the launches traced: 72.4 us -> 68.3 us
  Pallas kernels: 71.1 us -> 67 us
    pallas_call x1, Pallas kernels: 68.3 us -> 65.4 us  [per_device(): pl.pallas_call(kernel, out_shape=(pltpu.VMEM((NZ, NY, NX, ROWS, 128), BF1...]
    pallas_call x1, Pallas kernels: 2.82 us -> 1.61 us  [per_device(): pl.pallas_call(finish_kernel, out_shape=(jax.ShapeDtypeStruct((32, FF), B...]
where the time goes in v4:
time: 69.4 us; the launch traced here: 68.3 us
  Pallas kernels  67 us (97%)
  between operations  1.28 us (2%)
    pallas_call x1, Pallas kernels, per_device(): pl.pallas_call(kernel, out_shape=(pltpu.VMEM((NZ, NY, NX, ROWS, 128), BF1...  65.4 us
    pallas_call x1, Pallas kernels, per_device(): pl.pallas_call(finish_kernel, out_shape=(jax.ShapeDtypeStruct((32, FF), B...  1.61 us

profile of v4, /device:TPU:6, one launch (start us, length us, event | category | flops | bytes accessed | tf_op | source)
XLA Modules:
  0.0 68.3 jit_solution(359163369927096951)
XLA Ops:
  1.3 65.4 %shard_map.76 = (bf16[8,2,4,112,128]{4,3,2,1,0:T(8,128)(2,1)S(1)}, f32[112,128]{1,0:T(8,128)S(1)}, f32[8,128]{1,0:T(8,128)S(1)}) custom-call(bf16[16,4,112,128]{3,2,1,0:T(8,128)(2,1)} %bitcast.5, bf16[1,7168]{1,0:T(2,128)(2,1)} %scales.1, f32[1,1]{1,0:T(1,128)} %bitcast.3.clip, f32[112,128]{1,0:T(8,128)} %master.3, f32[112,128]{1,0:T(8,128)} %momentum.3), custom_call_target="tpu_custom_call" | custom-call | tf_op jit(solution)/shard_map/pallas_call | solution.py:392
  66.7 1.6 %shard_map.77 = (bf16[32,28672]{1,0:T(8,128)(2,1)}, f32[112,128]{1,0:T(8,128)}, f32[112,128]{1,0:T(8,128)}) custom-call(bf16[32,2,112,128]{3,2,1,0:T(8,128)(2,1)S(1)} %bitcast.4, f32[112,128]{1,0:T(8,128)S(1)} %get-tuple-element.7.grad, f32[8,128]{1,0:T(8,128)S(1)} %get-tuple-element.8.factor, f32[112,128]{1,0:T(8,128)} %master.3, f32[112,128]{1,0:T(8,128)} %momentum.3), custom_call_target="tpu_custom_call" | custom-call | tf_op jit(solution)/shard_map/pallas_call | solution.py:455

commit v5 on v4

--- a/solution.py
+++ b/solution.py
@@ -14,10 +14,12 @@
 PAD = 128
 EARLY = 96
 LATE = ROWS - EARLY
+FIRST, HALF = 88, 48
+LAST = ROWS - FIRST
 AHEAD = 6
 SEQUENCE = (
-    (0, 4), (0, 3), (0, 5), (1, 4), (0, 2), (0, 6), (1, 3), (1, 5),
-    (0, 1), (1, 2), (0, 7), (1, 6), (0, 0), (1, 1), (1, 7), (1, 0),
+    (0, 4), (0, 3), (0, 5), (1, 4), (0, 2), (1, 3), (0, 6), (1, 5),
+    (0, 1), (1, 2), (0, 7), (1, 6), (1, 1), (0, 0), (1, 7), (1, 0),
 )
 ALONG_ZC = tuple((0, 0, d, c) for c in (1, 0) for d in (4, 3, 5, 2, 6, 1, 7, 0))[:-1]
 ALONG_YX = tuple((dx, d, 0, 0) for dx in (2, 1, 3, 0) for d in (4, 3, 5, 2, 6, 1, 7, 0))[:-1]
@@ -142,15 +144,15 @@
             source = lax.rem(z + 8 - d, 8)
             block = blocks.at[source]
             copies.append(remote(block, block, send.at[i + 2], recv.at[i + 2], along_z(1 if d == 2 else 7)))
-            half = blocks.at[source, pl.ds(0 if d == 2 else EARLY // 2, EARLY // 2)]
+            half = blocks.at[source, pl.ds(0, HALF) if d == 2 else pl.ds(HALF, FIRST - HALF)]
             copies.append(remote(half, half, send.at[i + 4], recv.at[i + 4], along_z(d)))
         return copies[:2] + copies[4:]
 
     inputs[1].wait()
     inputs[2].wait()
     moved = master_v[...] - 0.567 * momentum_v[...]
-    az[z] = moved[:EARLY]
-    cx[yl, x, 0] = moved[EARLY:]
+    az[z] = moved[:FIRST]
+    cx[yl, x, 0] = moved[FIRST:]
 
     for zy in range(16):
         for k in range(4):
@@ -236,8 +238,8 @@
         late_total = late_total + xlrx[k]
     total = jnp.concatenate([total, late_total], axis=0)
     grad = total * (1.0 / (NX * NY * NZ))
-    gz[z] = grad[:EARLY]
-    cx[yl, x, 1] = grad[EARLY:]
+    gz[z] = grad[:FIRST]
+    cx[yl, x, 1] = grad[FIRST:]
     pl.semaphore_wait(heard.at[1], 4)
     partial = jnp.sum(grad * grad, axis=0, keepdims=True)
     for stage, ways in enumerate((ALONG_ZC, ALONG_YX)):
@@ -273,7 +275,7 @@
     for yy in range(NY):
         for xx in range(NX):
             nbc[yy, xx] = (cx[yy, xx, 0] - step * cx[yy, xx, 1]).astype(BF16)
-    here = gathered.at[z, :, :, pl.ds(EARLY, LATE)]
+    here = gathered.at[z, :, :, pl.ds(FIRST, LAST)]
     done = [
         remote(nbc, here, ds_.at[i], dr.at[i], along_z(d)) for i, d in enumerate((4, 3, 5, 2, 6, 1, 7))
     ]
@@ -282,9 +284,8 @@
     for copy in acopies + gcopies:
         copy.wait()
 
-    half = EARLY // 2
-    items_a = ((0, 0, EARLY), (1, 0, EARLY), (2, 0, EARLY), (3, 0, half))
-    items_b = ((4, 0, EARLY), (5, 0, EARLY), (6, 0, EARLY), (3, half, half), (7, 0, EARLY))
+    items_a = ((0, 0, FIRST), (1, 0, FIRST), (2, 0, FIRST), (3, 0, HALF))
+    items_b = ((4, 0, FIRST), (5, 0, FIRST), (6, 0, FIRST), (3, HALF, FIRST - HALF), (7, 0, FIRST))
     counter = [0]
 
     def base_to(item, yy, xx, to, first=False):
@@ -311,7 +312,7 @@
         b_y.append(base_to(items_b[i], yl, x, y_peer, True))
         if i < 4:
             a_x.append(both_ways(items_a[i], yl, True))
-    whole = pltpu.make_async_copy(nb, gathered.at[:, yl, x, pl.ds(0, EARLY)], own_sem)
+    whole = pltpu.make_async_copy(nb, gathered.at[:, yl, x, pl.ds(0, FIRST)], own_sem)
     whole.start()
     b_x, b_x2, a_far = [], [], []
     for i in range(5):
@@ -412,11 +413,11 @@
             pltpu.VMEM((NZ, EARLY, 128), F32),
             pltpu.VMEM((NZ - 1, EARLY, 128), F32),
             pltpu.VMEM((NZ - 1, EARLY, 128), F32),
-            pltpu.VMEM((NZ, EARLY, 128), F32),
-            pltpu.VMEM((NZ, EARLY, 128), F32),
-            pltpu.VMEM((NZ, EARLY, 128), BF16),
-            pltpu.VMEM((NY, NX, 2, LATE, 128), F32),
-            pltpu.VMEM((NY, NX, LATE, 128), BF16),
+            pltpu.VMEM((NZ, FIRST, 128), F32),
+            pltpu.VMEM((NZ, FIRST, 128), F32),
+            pltpu.VMEM((NZ, FIRST, 128), BF16),
+            pltpu.VMEM((NY, NX, 2, LAST, 128), F32),
+            pltpu.VMEM((NY, NX, LAST, 128), BF16),
             pltpu.VMEM((NY, NX, NZ * LATE, 128), BF16),
             pltpu.VMEM((NZ, NY * NX, 128), F32),
             pltpu.VMEM((NZ, NY * NX, 128), F32),

time: 69.4 us -> 68.2 us (0.983)
  Pallas kernels: 67 us -> 66.2 us
    pallas_call x1, Pallas kernels: 65.4 us -> 64.6 us  [per_device(): pl.pallas_call(kernel, out_shape=(pltpu.VMEM((NZ, NY, NX, ROWS, 128), BF1...]
where the time goes in v5:
time: 68.2 us; the launch traced here: 67.5 us
  Pallas kernels  66.2 us (97%)
  between operations  1.28 us (2%)
    pallas_call x1, Pallas kernels, per_device(): pl.pallas_call(kernel, out_shape=(pltpu.VMEM((NZ, NY, NX, ROWS, 128), BF1...  64.6 us
    pallas_call x1, Pallas kernels, per_device(): pl.pallas_call(finish_kernel, out_shape=(jax.ShapeDtypeStruct((32, FF), B...  1.61 us

profile of v5, /device:TPU:6, one launch (start us, length us, event | category | flops | bytes accessed | tf_op | source)
XLA Modules:
  0.0 67.5 jit_solution(6104816281867270520)
XLA Ops:
  1.3 64.6 %shard_map.76 = (bf16[8,2,4,112,128]{4,3,2,1,0:T(8,128)(2,1)S(1)}, f32[112,128]{1,0:T(8,128)S(1)}, f32[8,128]{1,0:T(8,128)S(1)}) custom-call(bf16[16,4,112,128]{3,2,1,0:T(8,128)(2,1)} %bitcast.5, bf16[1,7168]{1,0:T(2,128)(2,1)} %scales.1, f32[1,1]{1,0:T(1,128)} %bitcast.3.clip, f32[112,128]{1,0:T(8,128)} %master.3, f32[112,128]{1,0:T(8,128)} %momentum.3), custom_call_target="tpu_custom_call" | custom-call | tf_op jit(solution)/shard_map/pallas_call | solution.py:393
  65.9 1.6 %shard_map.77 = (bf16[32,28672]{1,0:T(8,128)(2,1)}, f32[112,128]{1,0:T(8,128)}, f32[112,128]{1,0:T(8,128)}) custom-call(bf16[32,2,112,128]{3,2,1,0:T(8,128)(2,1)S(1)} %bitcast.4, f32[112,128]{1,0:T(8,128)S(1)} %get-tuple-element.7.grad, f32[8,128]{1,0:T(8,128)S(1)} %get-tuple-element.8.factor, f32[112,128]{1,0:T(8,128)} %master.3, f32[112,128]{1,0:T(8,128)} %momentum.3), custom_call_target="tpu_custom_call" | custom-call | tf_op jit(solution)/shard_map/pallas_call | solution.py:456

commit v6 on v5

--- a/solution.py
+++ b/solution.py
@@ -16,7 +16,7 @@
 LATE = ROWS - EARLY
 FIRST, HALF = 88, 48
 LAST = ROWS - FIRST
-AHEAD = 6
+AHEAD = 8
 SEQUENCE = (
     (0, 4), (0, 3), (0, 5), (1, 4), (0, 2), (1, 3), (0, 6), (1, 5),
     (0, 1), (1, 2), (0, 7), (1, 6), (1, 1), (0, 0), (1, 7), (1, 0),
@@ -99,7 +99,7 @@
             for k, d in enumerate((2, 1, 3))
         ]
 
-    xcopies = [send_along_x(0), send_along_x(1)]
+    xcopies = [send_along_x(s) for s in range(3)]
     for d in (1, 2, 6, 7):
         for way in ((0, d, 0, 0), (0, 0, d, 0)):
             pl.semaphore_signal(heard.at[0], inc=1, device_id=partner(way), device_id_type=MESH)
@@ -113,7 +113,7 @@
         remote(table16.at[lax.rem(x + d, 4)], rs.at[x], ss.at[k], sr.at[k], along_x(d))
         for k, d in enumerate((2, 1, 3))
     ]
-    for s in range(2, AHEAD):
+    for s in range(3, AHEAD):
         xcopies.append(send_along_x(s))
     lanes = lax.broadcasted_iota(jnp.int32, (NZ * NY, 128), 1) // LATE == z
     for k in range(4):

time: 68.2 us -> 69.5 us (1.019)
  Pallas kernels: 66.2 us -> 67.4 us
    pallas_call x1, Pallas kernels: 64.6 us -> 65.8 us  [per_device(): pl.pallas_call(kernel, out_shape=(pltpu.VMEM((NZ, NY, NX, ROWS, 128), BF1...]
where the time goes in v6:
time: 69.5 us; the launch traced here: 68.7 us
  Pallas kernels  67.4 us (97%)
  between operations  1.28 us (2%)
    pallas_call x1, Pallas kernels, per_device(): pl.pallas_call(kernel, out_shape=(pltpu.VMEM((NZ, NY, NX, ROWS, 128), BF1...  65.8 us
    pallas_call x1, Pallas kernels, per_device(): pl.pallas_call(finish_kernel, out_shape=(jax.ShapeDtypeStruct((32, FF), B...  1.61 us

profile of v6, /device:TPU:6, one launch (start us, length us, event | category | flops | bytes accessed | tf_op | source)
XLA Modules:
  0.0 68.7 jit_solution(11041974185487611097)
XLA Ops:
  1.3 65.8 %shard_map.76 = (bf16[8,2,4,112,128]{4,3,2,1,0:T(8,128)(2,1)S(1)}, f32[112,128]{1,0:T(8,128)S(1)}, f32[8,128]{1,0:T(8,128)S(1)}) custom-call(bf16[16,4,112,128]{3,2,1,0:T(8,128)(2,1)} %bitcast.5, bf16[1,7168]{1,0:T(2,128)(2,1)} %scales.1, f32[1,1]{1,0:T(1,128)} %bitcast.3.clip, f32[112,128]{1,0:T(8,128)} %master.3, f32[112,128]{1,0:T(8,128)} %momentum.3), custom_call_target="tpu_custom_call" | custom-call | tf_op jit(solution)/shard_map/pallas_call | solution.py:393
  67.1 1.6 %shard_map.77 = (bf16[32,28672]{1,0:T(8,128)(2,1)}, f32[112,128]{1,0:T(8,128)}, f32[112,128]{1,0:T(8,128)}) custom-call(bf16[32,2,112,128]{3,2,1,0:T(8,128)(2,1)S(1)} %bitcast.4, f32[112,128]{1,0:T(8,128)S(1)} %get-tuple-element.7.grad, f32[8,128]{1,0:T(8,128)S(1)} %get-tuple-element.8.factor, f32[112,128]{1,0:T(8,128)} %master.3, f32[112,128]{1,0:T(8,128)} %momentum.3), custom_call_target="tpu_custom_call" | custom-call | tf_op jit(solution)/shard_map/pallas_call | solution.py:456
